TPU v7x, 32 devices: a whole 2x2x4 slice. The times are simulated.
32 devices in a mesh: groups: 2 (over y), ctx: 16 (over z, x, core).
Axes of the slice: x: 2, y: 2, z: 4, core: 2. Of those that a mesh axis runs over, the one named last changes fastest.
Arguments:
- queries: bfloat16 [8192, 4096], P(('groups', 'ctx')), parts along dimension 0, may hold values from -13 to 13
- all_key_states: bfloat16 [8192, 512], P(('groups', 'ctx')), parts along dimension 0, may hold values from -9.5 to 9.5
- all_value_states: bfloat16 [8192, 512], P(('groups', 'ctx')), parts along dimension 0, may hold values from -6 to 6
- selected: int32 [32, 2], P(('groups', 'ctx')), parts along dimension 0, may hold values from 0 to 14, as said below
Outputs:
- attended: bfloat16 [8192, 4096], P(('groups', 'ctx')), parts along dimension 0
There are 2 independent parts, one for each index of `groups`. A program takes and returns all parts, laid end to end along the dimension named above; each array names one. Nothing has to cross between parts.
Inputs may be any that keep to these rules, and one draw needn't show every extreme that they name: `selected`: for block i >= 2 the two entries of row i are different blocks below i; rows 0 and 1 hold 0 and 0; the last block's first entry is 14.
All inputs are finite; a program needn't handle non-finite values.
Results may differ from a plain program's by a relative error of at most 0.004.
Values may be sent and summed in bfloat16 or wider, within the bound.
A program may use at most 64 MiB of HBM per device.

v0:
```python
import math

import jax
import jax.numpy as jnp
from jax import lax
from jax.sharding import PartitionSpec as P

QUERY_HEADS = 32
KEY_VALUE_HEADS = 4
HEAD_SIZE = 128


def attend(query_head_count, key_head_count, value_heads, allowed):
    score_scale = 1.0 / math.sqrt(query_head_count.shape[-1])

    def one_head(operands):
        query_part, key_part, value_part = operands
        scores = (
            jnp.einsum("trd,ud->tru", query_part, key_part, preferred_element_type=jnp.float32)
            * score_scale
        )
        scores = jnp.where(allowed[:, None, :], scores, jnp.float32(-1e30))
        row_max = jnp.max(scores, axis=2, keepdims=True)
        weights = jnp.exp(scores - row_max)
        row_sum = jnp.sum(weights, axis=2, keepdims=True)
        mixture = jnp.einsum(
            "tru,ud->trd",
            weights.astype(jnp.bfloat16),
            value_part,
            preferred_element_type=jnp.float32,
        )
        return (mixture / row_sum).astype(jnp.bfloat16)

    stacked = lax.map(
        one_head,
        (
            query_head_count.transpose(1, 0, 2, 3),
            key_head_count.transpose(1, 0, 2),
            value_heads.transpose(1, 0, 2),
        ),
    )
    return stacked.transpose(1, 0, 2, 3)


def local(queries, all_key_states, all_value_states, selected):
    devices = lax.axis_size("ctx")
    my_block = lax.axis_index("ctx")
    block_row_count, feature_width = all_key_states.shape
    piece_rows = block_row_count // devices
    key_split = all_key_states.reshape(devices, piece_rows, feature_width)
    value_split = all_value_states.reshape(devices, piece_rows, feature_width)
    requests = lax.all_gather(selected, "ctx", axis=0, tiled=True)
    held_keys, held_values = (
        lax.all_to_all(key_split, "ctx", split_axis=0, concat_axis=0, tiled=True),
        lax.all_to_all(value_split, "ctx", split_axis=0, concat_axis=0, tiled=True),
    )
    wanted = requests.T
    first_keys, first_values = (
        lax.all_to_all(
            jnp.take(held_keys, wanted[0], axis=0), "ctx", split_axis=0, concat_axis=0, tiled=True
        ),
        lax.all_to_all(
            jnp.take(held_values, wanted[0], axis=0), "ctx", split_axis=0, concat_axis=0, tiled=True
        ),
    )
    second_keys, second_values = (
        lax.all_to_all(
            jnp.take(held_keys, wanted[1], axis=0), "ctx", split_axis=0, concat_axis=0, tiled=True
        ),
        lax.all_to_all(
            jnp.take(held_values, wanted[1], axis=0), "ctx", split_axis=0, concat_axis=0, tiled=True
        ),
    )
    distant_keys = jnp.concatenate(
        [
            first_keys.reshape(block_row_count, feature_width),
            second_keys.reshape(block_row_count, feature_width),
        ],
        axis=0,
    )
    remote_values = jnp.concatenate(
        [
            first_values.reshape(block_row_count, feature_width),
            second_values.reshape(block_row_count, feature_width),
        ],
        axis=0,
    )
    first_block = selected[0, 0]
    second_block = selected[0, 1]
    first_valid = first_block < my_block
    second_valid = jnp.logical_and(second_block < my_block, second_block != first_block)
    row_ids = jnp.arange(block_row_count, dtype=jnp.int32)
    causal = row_ids[None, :] <= row_ids[:, None]
    allowed = jnp.concatenate(
        [
            causal,
            jnp.broadcast_to(first_valid, (block_row_count, block_row_count)),
            jnp.broadcast_to(second_valid, (block_row_count, block_row_count)),
        ],
        axis=1,
    )
    key_head_count = jnp.concatenate([all_key_states, distant_keys], axis=0).reshape(
        3 * block_row_count, KEY_VALUE_HEADS, HEAD_SIZE
    )
    value_heads = jnp.concatenate([all_value_states, remote_values], axis=0).reshape(
        3 * block_row_count, KEY_VALUE_HEADS, HEAD_SIZE
    )
    query_head_count = queries.reshape(
        block_row_count, KEY_VALUE_HEADS, QUERY_HEADS // KEY_VALUE_HEADS, HEAD_SIZE
    )
    attended = attend(query_head_count, key_head_count, value_heads, allowed)
    return attended.reshape(block_row_count, QUERY_HEADS * HEAD_SIZE)


def solution(mesh):
    placed = (
        P(("groups", "ctx"), None),
        P(("groups", "ctx"), None),
        P(("groups", "ctx"), None),
        P(("groups", "ctx"), None),
    )
    return jax.shard_map(
        local, mesh=mesh, in_specs=placed, out_specs=P(("groups", "ctx"), None), check_vma=False
    )
```

profile of v0, /device:TPU:25, one launch (start us, length us, event | category | flops | bytes accessed | tf_op | source)
XLA Modules:
  0.0 135.3 jit_solution(8048211730979571622)
XLA Ops:
  0.0 13.9 %all_to_all.30 = bf16[16,16,512]{2,1,0:T(8,128)(2,1)S(1)} all-to-all(bf16[16,16,512]{2,1,0:T(8,128)(2,1)} %bitcast.63), channel_id=1, replica_groups=mesh['groups'=2,'ctx'=16] {'ctx'}, dimensions={0} | all-to-all | bytes 524288 | tf_op jit(solution)/shard_map/all_to_all | solution.py:54
  13.9 6.0 %all-to-all-start.3 = ((bf16[16,16,512]{2,1,0:T(8,128)(2,1)}), bf16[16,16,512]{2,1,0:T(8,128)(2,1)S(1)}, u32[]{:S(2)}, u32[]{:S(2)}) async-start(bf16[16,16,512]{2,1,0:T(8,128)(2,1)} %bitcast.64), calls=%async_computation.3 | async-start | bytes 524288 | tf_op jit(solution)/shard_map/all_to_all | solution.py:55
  19.9 17.3 %all-gather = s32[16,1,2]{2,1,0:T(1,128)S(1)} all-gather(s32[1,1,2]{2,1,0:T(1,128)} %bitcast.65), channel_id=1, replica_groups=mesh['groups'=2,'ctx'=16] {'ctx'}, dimensions={0}, use_global_device_ids=true | all-gather | bytes 136 | tf_op jit(solution)/shard_map/all_gather | solution.py:52
  37.1 0.1 copy.21
  37.3 0.6 gather_fusion
  37.8 0.0 all-to-all-done.3
  37.8 0.6 gather_fusion.2
  38.4 0.8 broadcast_select_fusion.2
  39.2 8.2 %all-to-all-start.1 = ((bf16[16,16,512]{2,1,0:T(8,128)(2,1)}), bf16[16,16,512]{2,1,0:T(8,128)(2,1)S(1)}, u32[]{:S(2)}, u32[]{:S(2)}) async-start(bf16[16,16,512]{2,1,0:T(8,128)(2,1)} %get-tuple-element.72), calls=%async_computation.1 | async-start | bytes 524288 | tf_op jit(solution)/shard_map/all_to_all | solution.py:59
  47.4 0.0 copy-start.1
  47.4 0.6 gather_fusion.1
  48.0 0.0 copy-start.2
  48.0 0.6 gather_fusion.3
  48.6 0.8 broadcast_select_fusion
  49.4 5.4 %all-to-all-done.1 = bf16[16,16,512]{2,1,0:T(8,128)(2,1)S(1)} async-done(((bf16[16,16,512]{2,1,0:T(8,128)(2,1)}), bf16[16,16,512]{2,1,0:T(8,128)(2,1)S(1)}, u32[]{:S(2)}, u32[]{:S(2)}) %all-to-all-start.1) | async-done | bytes 262176 | tf_op jit(solution)/shard_map/all_to_all | solution.py:59
  54.8 13.3 %all_to_all.31 = bf16[16,16,512]{2,1,0:T(8,128)(2,1)} all-to-all(bf16[16,16,512]{2,1,0:T(8,128)(2,1)S(1)} %get-tuple-element.74), channel_id=1, replica_groups=mesh['groups'=2,'ctx'=16] {'ctx'}, dimensions={0} | all-to-all | bytes 524288 | tf_op jit(solution)/shard_map/all_to_all | solution.py:67
  68.1 12.9 %all_to_all.32 = bf16[16,16,512]{2,1,0:T(8,128)(2,1)S(1)} all-to-all(bf16[16,16,512]{2,1,0:T(8,128)(2,1)S(1)} %get-tuple-element.71), channel_id=1, replica_groups=mesh['groups'=2,'ctx'=16] {'ctx'}, dimensions={0} | all-to-all | bytes 524288 | tf_op jit(solution)/shard_map/all_to_all | solution.py:62
  81.0 6.0 %all-to-all-start.5 = ((bf16[16,16,512]{2,1,0:T(8,128)(2,1)}), bf16[16,16,512]{2,1,0:T(8,128)(2,1)S(1)}, u32[]{:S(2)}, u32[]{:S(2)}) async-start(bf16[16,16,512]{2,1,0:T(8,128)(2,1)} %get-tuple-element.73), calls=%async_computation.5 | async-start | bytes 524288 | tf_op jit(solution)/shard_map/all_to_all | solution.py:70
  87.0 0.1 copy.20
  87.2 0.8 copy.24
  88.0 0.6 fusion.25
  91.1 3.3 %copy.19 = bf16[256,4096]{0,1:T(8,128)(2,1)S(1)} copy(bf16[256,4096]{1,0:T(8,128)(2,1)} %param.8) | data formatting | bytes 4194304 | tf_op args[0]
  94.5 0.1 add_add_fusion
  94.5 0.8 concatenate.25
  95.3 1.8 %copy.22 = bf16[256,4,128]{0,2,1:T(8,128)(2,1)} copy(bf16[256,4,128]{2,1,0:T(4,128)(2,1)} %concatenate.25) | data formatting | bytes 524288 | tf_op jit(solution)/shard_map/concatenate | solution.py:102
  97.1 1.0 concatenate.26
  98.1 0.9 copy.23
  99.0 0.1 concatenate.29
  99.1 0.9 copy.25
  100.0 0.0 all-to-all-done.5
  100.0 0.1 concatenate.30
  100.1 0.9 copy.26
  101.0 2.3 %maximum_bitcast_fusion = (bf16[4,768,128]{1,2,0:T(8,128)(2,1)S(1)}, bf16[4,768,128]{1,2,0:T(8,128)(2,1)}) fusion(bf16[256,4,128]{0,2,1:T(8,128)(2,1)} %copy.23, bf16[256,4,128]{0,2,1:T(8,128)(2,1)} %copy.22, bf16[256,4,128]{0,2,1:T(8,128)(2,1)S(1)} %bitcast.61, bf16[256,4,128]{0,2,1:T(8,128)(2,1)} %copy.26, bf16[256,4,128]{0,2,1:T(8,128)(2,1)} %copy.25, ...), kind=kLoop, calls=%fused_computation.26 | loop fusion | flops 4718592 | bytes 3145728 | tf_op jit(solution)/shard_map/transpose | solution.py:38
  103.2 26.9 %while.10 = (s32[]{:T(128)}, bf16[4,256,8,128]{3,1,2,0:T(8,128)(2,1)}, pred[256,768]{1,0:T(8,128)(4,1)S(1)}, bf16[4,256,8,128]{1,3,2,0:T(8,128)(2,1)S(1)}, bf16[...) while((s32[]{:T(128)}, bf16[4,256,8,128]{3,1,2,0:T(8,128)(2,1)}, ...), condition=%wide.region_3.5_spmd, body=%wide.region_0.4_spmd.sunk | while | flops 823128064 | bytes 20949068 | solution.py:34
  103.2 1.3 fusion.33
  104.6 1.7 %fusion.34 = f32[256,8]{0,1:T(8,128)S(1)} fusion(f32[256,8,768]{2,0,1:T(8,128)S(1)} %get-tuple-element.118, f32[256,8]{0,1:T(8,128)S(1)} %get-tuple-element.119, pred[256,768]{1,0:T(8,128)(4,1)S(1)} %get-tuple-element.136), kind=kLoop, calls=%fused_computation.7.clone.1 | loop fusion | flops 6289408 | bytes 6504448 | tf_op jit(solution)/shard_map/while/body/eval_jaxpr/reduce_sum | solution.py:25
  106.2 3.7 %fusion.35 = bf16[4,256,8,128]{3,1,2,0:T(8,128)(2,1)} fusion(bf16[4,256,8,128]{3,1,2,0:T(8,128)(2,1)} %get-tuple-element.128, s32[]{:T(128)} %get-tuple-element.127, f32[256,8,768]{2,0,1:T(8,128)S(1)} %get-tuple-element.118, f32[256,8]{0,1:T(8,128)S(1)} %get-tuple-element.119, pred[256,768]{1,0:T(8,128)(4,1)S(1)} %get-tuple-element.136, ...), kind=kOutput, calls=%fused_computation.13.clone.1 | convolution fusion | flops 409468928 | bytes 7226368 | tf_op jit(solution)/shard_map/while/body/eval_jaxpr/tru,ud->trd/dot_general | solution.py:26
  109.9 1.3 fusion.33
  111.3 1.7 %fusion.34 = f32[256,8]{0,1:T(8,128)S(1)} fusion(f32[256,8,768]{2,0,1:T(8,128)S(1)} %get-tuple-element.118, f32[256,8]{0,1:T(8,128)S(1)} %get-tuple-element.119, pred[256,768]{1,0:T(8,128)(4,1)S(1)} %get-tuple-element.136), kind=kLoop, calls=%fused_computation.7.clone.1 | loop fusion | flops 6289408 | bytes 6504448 | tf_op jit(solution)/shard_map/while/body/eval_jaxpr/reduce_sum | solution.py:25
  113.0 3.7 %fusion.35 = bf16[4,256,8,128]{3,1,2,0:T(8,128)(2,1)} fusion(bf16[4,256,8,128]{3,1,2,0:T(8,128)(2,1)} %get-tuple-element.128, s32[]{:T(128)} %get-tuple-element.127, f32[256,8,768]{2,0,1:T(8,128)S(1)} %get-tuple-element.118, f32[256,8]{0,1:T(8,128)S(1)} %get-tuple-element.119, pred[256,768]{1,0:T(8,128)(4,1)S(1)} %get-tuple-element.136, ...), kind=kOutput, calls=%fused_computation.13.clone.1 | convolution fusion | flops 409468928 | bytes 7226368 | tf_op jit(solution)/shard_map/while/body/eval_jaxpr/tru,ud->trd/dot_general | solution.py:26
  116.7 1.3 fusion.33
  118.0 1.7 %fusion.34 = f32[256,8]{0,1:T(8,128)S(1)} fusion(f32[256,8,768]{2,0,1:T(8,128)S(1)} %get-tuple-element.118, f32[256,8]{0,1:T(8,128)S(1)} %get-tuple-element.119, pred[256,768]{1,0:T(8,128)(4,1)S(1)} %get-tuple-element.136), kind=kLoop, calls=%fused_computation.7.clone.1 | loop fusion | flops 6289408 | bytes 6504448 | tf_op jit(solution)/shard_map/while/body/eval_jaxpr/reduce_sum | solution.py:25
  119.7 3.7 %fusion.35 = bf16[4,256,8,128]{3,1,2,0:T(8,128)(2,1)} fusion(bf16[4,256,8,128]{3,1,2,0:T(8,128)(2,1)} %get-tuple-element.128, s32[]{:T(128)} %get-tuple-element.127, f32[256,8,768]{2,0,1:T(8,128)S(1)} %get-tuple-element.118, f32[256,8]{0,1:T(8,128)S(1)} %get-tuple-element.119, pred[256,768]{1,0:T(8,128)(4,1)S(1)} %get-tuple-element.136, ...), kind=kOutput, calls=%fused_computation.13.clone.1 | convolution fusion | flops 409468928 | bytes 7226368 | tf_op jit(solution)/shard_map/while/body/eval_jaxpr/tru,ud->trd/dot_general | solution.py:26
  123.4 1.3 fusion.33
  124.7 1.7 %fusion.34 = f32[256,8]{0,1:T(8,128)S(1)} fusion(f32[256,8,768]{2,0,1:T(8,128)S(1)} %get-tuple-element.118, f32[256,8]{0,1:T(8,128)S(1)} %get-tuple-element.119, pred[256,768]{1,0:T(8,128)(4,1)S(1)} %get-tuple-element.136), kind=kLoop, calls=%fused_computation.7.clone.1 | loop fusion | flops 6289408 | bytes 6504448 | tf_op jit(solution)/shard_map/while/body/eval_jaxpr/reduce_sum | solution.py:25
  126.4 3.7 %fusion.35 = bf16[4,256,8,128]{3,1,2,0:T(8,128)(2,1)} fusion(bf16[4,256,8,128]{3,1,2,0:T(8,128)(2,1)} %get-tuple-element.128, s32[]{:T(128)} %get-tuple-element.127, f32[256,8,768]{2,0,1:T(8,128)S(1)} %get-tuple-element.118, f32[256,8]{0,1:T(8,128)S(1)} %get-tuple-element.119, pred[256,768]{1,0:T(8,128)(4,1)S(1)} %get-tuple-element.136, ...), kind=kOutput, calls=%fused_computation.13.clone.1 | convolution fusion | flops 409468928 | bytes 7226368 | tf_op jit(solution)/shard_map/while/body/eval_jaxpr/tru,ud->trd/dot_general | solution.py:26
  130.1 2.9 %copy.30 = bf16[256,4,8,128]{3,2,1,0:T(8,128)(2,1)S(1)} copy(bf16[256,4,8,128]{3,0,2,1:T(8,128)(2,1)} %bitcast.22) | data formatting | bytes 4194304 | tf_op jit(solution)/shard_map/transpose | solution.py:42
  133.0 2.3 %copy.36 = bf16[32,8,32,128]{3,1,2,0:T(8,128)(2,1)} copy(bf16[32,8,32,128]{3,2,1,0:T(8,128)(2,1)S(1)} %bitcast.60) | data formatting | bytes 4194304
  (13 shorter events, 0.1 us)
Async XLA Ops:
  13.9 24.0 %all-to-all-start.3 = ((bf16[16,16,512]{2,1,0:T(8,128)(2,1)}), bf16[16,16,512]{2,1,0:T(8,128)(2,1)S(1)}, u32[]{:S(2)}, u32[]{:S(2)}) async-start(bf16[16,16,512]{2,1,0:T(8,128)(2,1)} %bitcast.64), calls=%async_computation.3 | async-start | bytes 524288 | tf_op jit(solution)/shard_map/all_to_all | solution.py:55
  39.2 47.8 %copy-start = (bf16[256,512]{1,0:T(8,128)(2,1)S(1)}, bf16[256,512]{1,0:T(8,128)(2,1)}, u32[]{:S(2)}) copy-start(bf16[256,512]{1,0:T(8,128)(2,1)} %param.9) | copy-start | bytes 786436
  39.2 15.6 %all-to-all-start.1 = ((bf16[16,16,512]{2,1,0:T(8,128)(2,1)}), bf16[16,16,512]{2,1,0:T(8,128)(2,1)S(1)}, u32[]{:S(2)}, u32[]{:S(2)}) async-start(bf16[16,16,512]{2,1,0:T(8,128)(2,1)} %get-tuple-element.72), calls=%async_computation.1 | async-start | bytes 524288 | tf_op jit(solution)/shard_map/all_to_all | solution.py:59
  47.4 39.8 %copy-start.1 = (bf16[256,512]{1,0:T(8,128)(2,1)S(1)}, bf16[256,512]{1,0:T(8,128)(2,1)}, u32[]{:S(2)}) copy-start(bf16[256,512]{1,0:T(8,128)(2,1)} %param.10) | copy-start | bytes 786436
  48.0 40.1 %copy-start.2 = (s32[1,2]{1,0:T(1,128)S(1)}, s32[1,2]{1,0:T(1,128)}, u32[]{:S(2)}) copy-start(s32[1,2]{1,0:T(1,128)} %param.11) | copy-start | bytes 28
  81.0 19.0 %all-to-all-start.5 = ((bf16[16,16,512]{2,1,0:T(8,128)(2,1)}), bf16[16,16,512]{2,1,0:T(8,128)(2,1)S(1)}, u32[]{:S(2)}, u32[]{:S(2)}) async-start(bf16[16,16,512]{2,1,0:T(8,128)(2,1)} %get-tuple-element.73), calls=%async_computation.5 | async-start | bytes 524288 | tf_op jit(solution)/shard_map/all_to_all | solution.py:70
where the time goes:
time: 137 us; the launch traced here: 135 us
  blocking collectives  57.3 us (42%)
  starting transfers between devices  20.2 us (15%)
  matrix products  20.1 us (15%)
  local copies, waits for them, and re-layouts  18.8 us (14%)
  other arithmetic  10.7 us (8%)
  waiting for transfers between devices  5.45 us (4%)
  between operations  2.63 us (2%)
    all_gather x1, blocking collectives, local(): requests = lax.all_gather(selected, 'ctx', axis=0, tiled=True)  17.3 us
    dot_general x4, matrix products, one_head(): jnp.einsum('tru,ud->trd', weights.astype(jnp.bfloat16), value_part, prefe...  14.8 us
    all_to_all x1, blocking collectives, local(): lax.all_to_all(key_split, 'ctx', split_axis=0, concat_axis=0, tiled=True)  13.9 us
    all_to_all x1, blocking collectives, local(): lax.all_to_all(jnp.take(held_keys, wanted[1], axis=0), 'ctx', split_axis=...  13.3 us
    all_to_all x1, blocking collectives, local(): lax.all_to_all(jnp.take(held_values, wanted[0], axis=0), 'ctx', split_axi...  12.9 us
    all_to_all x1, starting transfers between devices, local(): lax.all_to_all(jnp.take(held_keys, wanted[0], axis=0), 'ctx', split_axis=...  8.15 us
    reduce_sum x4, other arithmetic, one_head(): row_sum = jnp.sum(weights, axis=2, keepdims=True)  6.7 us
    unnamed x10, local copies, waits for them, and re-layouts  6.56 us
  transfers between devices with their start and end apart: 3, of which 1 were waited for; matrix products, arithmetic and copies ran while one was open for 10% of the time, Pallas kernels for 0%

commit v1 on v0

v1 whole, which is shorter than its diff:
```python
import functools
import math

import jax
import jax.numpy as jnp
from jax import lax
from jax.experimental import pallas as pl
from jax.experimental.pallas import tpu as pltpu
from jax.sharding import PartitionSpec as P

QUERY_HEADS = 32
KEY_VALUE_HEADS = 4
HEAD_SIZE = 128
GROUP_WIDTH = QUERY_HEADS // KEY_VALUE_HEADS
EXPONENT_SCALE = math.log2(math.e) / math.sqrt(HEAD_SIZE)
MASKED = -1e30
LAYERS = 4
SIDE = 4
MESH = pl.DeviceIdType.MESH


def attend_head(queries, keys, values, causal, first_valid, second_valid, rows):
    scores = lax.dot_general(
        queries, keys, (((1,), (1,)), ((), ())), preferred_element_type=jnp.float32
    )
    own = jnp.where(causal, scores[:, :rows], MASKED)
    first = scores[:, rows : 2 * rows]
    second = scores[:, 2 * rows :]
    own_max = jnp.max(own, axis=1, keepdims=True)
    first_max = jnp.where(first_valid, jnp.max(first, axis=1, keepdims=True), MASKED)
    second_max = jnp.where(second_valid, jnp.max(second, axis=1, keepdims=True), MASKED)
    row_max = jnp.maximum(own_max, jnp.maximum(first_max, second_max))
    own = jnp.exp2((own - row_max) * EXPONENT_SCALE)
    first = jnp.exp2((first - jnp.where(first_valid, row_max, -MASKED)) * EXPONENT_SCALE)
    second = jnp.exp2((second - jnp.where(second_valid, row_max, -MASKED)) * EXPONENT_SCALE)
    row_sum = jnp.sum(own + first + second, axis=1, keepdims=True)
    weights = jnp.concatenate(
        [own.astype(jnp.bfloat16), first.astype(jnp.bfloat16), second.astype(jnp.bfloat16)], axis=1
    )
    mixture = jnp.dot(weights, values, preferred_element_type=jnp.float32)
    return (mixture * (1.0 / row_sum)).astype(jnp.bfloat16)


def relay_kernel(
    rows,
    selected_ref,
    query_ref,
    key_ref,
    value_ref,
    out_ref,
    *scratch,
):
    heads = KEY_VALUE_HEADS
    stores = scratch[:heads]
    gathered = scratch[heads : 2 * heads]
    upward = scratch[2 * heads : 3 * heads]
    outgoing = scratch[3 * heads : 4 * heads]
    (
        request_vmem,
        request_smem,
        request_send,
        request_recv,
        spread_send,
        spread_recv,
        chain_send,
        chain_recv,
        deliver_send,
        deliver_recv,
        local_sem,
    ) = scratch[4 * heads :]
    quarter = rows // SIDE
    me = lax.axis_index("ctx")
    layer = me // SIDE
    place = me % SIDE

    def peer(offset):
        return layer * SIDE + (place + offset) % SIDE

    for g in range(heads):
        columns = slice(g * HEAD_SIZE, (g + 1) * HEAD_SIZE)
        gathered[g][0, 0] = key_ref[:, columns]
        gathered[g][1, 0] = value_ref[:, columns]
    lane = lax.broadcasted_iota(jnp.int32, (1, 128), 1)
    request_vmem[place] = jnp.where(lane == 0, selected_ref[0, 0], selected_ref[0, 1])

    barrier = pltpu.get_barrier_semaphore()
    for offset in range(1, SIDE):
        pl.semaphore_signal(barrier, inc=1, device_id={"ctx": peer(offset)}, device_id_type=MESH)

    @pl.when(layer > 0)
    def _():
        for q in range(SIDE):
            pl.semaphore_signal(
                barrier, inc=1, device_id={"ctx": (layer - 1) * SIDE + q}, device_id_type=MESH
            )

    @pl.when(layer < LAYERS - 1)
    def _():
        for q in range(SIDE):
            pl.semaphore_signal(
                barrier, inc=1, device_id={"ctx": (layer + 1) * SIDE + q}, device_id_type=MESH
            )

    neighbour_layers = jnp.minimum(layer, 1) + jnp.minimum(LAYERS - 1 - layer, 1)
    pl.semaphore_wait(barrier, SIDE - 1 + SIDE * neighbour_layers)

    def spread(g, offset):
        target = (place + offset) % SIDE
        return pltpu.make_async_remote_copy(
            src_ref=gathered[g].at[:, 0, pl.ds(target * quarter, quarter), :],
            dst_ref=stores[g].at[me],
            send_sem=spread_send.at[g, offset - 1],
            recv_sem=spread_recv.at[g, offset - 1],
            device_id={"ctx": peer(offset)},
            device_id_type=MESH,
        )

    def request(offset):
        return pltpu.make_async_remote_copy(
            src_ref=request_vmem.at[place],
            dst_ref=request_vmem.at[place],
            send_sem=request_send.at[offset - 1],
            recv_sem=request_recv.at[offset - 1],
            device_id={"ctx": peer(offset)},
            device_id_type=MESH,
        )

    def request_down(offset):
        return pltpu.make_async_remote_copy(
            src_ref=request_vmem.at[place],
            dst_ref=request_vmem.at[SIDE + place],
            send_sem=request_send.at[SIDE - 1 + offset],
            recv_sem=request_recv.at[SIDE - 1 + offset],
            device_id={"ctx": (LAYERS - 2) * SIDE + (place + offset) % SIDE},
            device_id_type=MESH,
        )

    def chain(g, source_layer, slot):
        part = stores[g].at[pl.ds(source_layer * SIDE, SIDE)]
        return pltpu.make_async_remote_copy(
            src_ref=part,
            dst_ref=part,
            send_sem=chain_send.at[g, slot],
            recv_sem=chain_recv.at[g, slot],
            device_id={"ctx": (layer + 1) % LAYERS * SIDE + place},
            device_id_type=MESH,
        )

    def chain_top(g):
        return pltpu.make_async_remote_copy(
            src_ref=upward[g].at[pl.ds(0, 2 * SIDE - 1)],
            dst_ref=stores[g].at[pl.ds(0, 2 * SIDE - 1)],
            send_sem=chain_send.at[g, 0],
            recv_sem=chain_recv.at[g, 0],
            device_id={"ctx": (LAYERS - 1) * SIDE + place},
            device_id_type=MESH,
        )

    def deliver(g, offset):
        return pltpu.make_async_remote_copy(
            src_ref=outgoing[g].at[offset - 1],
            dst_ref=gathered[g].at[:, pl.ds(1, 2), pl.ds(place * quarter, quarter), :],
            send_sem=deliver_send.at[g, offset - 1],
            recv_sem=deliver_recv.at[g, offset - 1],
            device_id={"ctx": peer(offset)},
            device_id_type=MESH,
        )

    for offset in range(1, SIDE):
        request(offset).start()

    @pl.when(layer == LAYERS - 1)
    def _():
        for offset in range(SIDE):
            request_down(offset).start()

    for g in range(heads):
        for offset in range(1, SIDE):
            spread(g, offset).start()
        stores[g][me] = gathered[g][:, 0, pl.ds(place * quarter, quarter), :]

    for offset in range(1, SIDE):
        request(offset).wait_recv()

    @pl.when(layer == LAYERS - 2)
    def _():
        for offset in range(SIDE):
            request_down(offset).wait_recv()

    @pl.when(layer != LAYERS - 2)
    def _():
        for q in range(SIDE):
            request_vmem[SIDE + q] = jnp.zeros((1, 128), jnp.int32)

    to_smem = pltpu.make_async_copy(request_vmem, request_smem, local_sem)
    to_smem.start()
    to_smem.wait()

    first_valid = selected_ref[0, 0] < me
    second_valid = jnp.logical_and(
        selected_ref[0, 1] < me, selected_ref[0, 1] != selected_ref[0, 0]
    )
    causal = lax.broadcasted_iota(jnp.int32, (rows, rows), 1) <= lax.broadcasted_iota(
        jnp.int32, (rows, rows), 0
    )

    def wait_spread(g):
        for offset in range(1, SIDE):
            spread(g, offset).wait_recv()

    def pass_on(g):
        @pl.when(layer == 0)
        def _():
            chain(g, 0, 0).start()

        @pl.when(layer == 1)
        def _():
            chain(g, 1, 0).start()
            chain(g, 0, 0).wait_recv()
            chain(g, 0, 1).start()

        @pl.when(layer == 2)
        def _():
            chain(g, 1, 0).wait_recv()
            chain(g, 0, 1).wait_recv()
            for slot in range(2 * SIDE - 1):
                wanted = request_smem[SIDE + slot % SIDE, 0, 1 - slot // SIDE]
                upward[g][slot] = stores[g][jnp.minimum(wanted, (LAYERS - 1) * SIDE - 1)]
            chain_top(g).start()

        @pl.when(layer == LAYERS - 1)
        def _():
            chain_top(g).wait_recv()

    def hand_out(g):
        def wanted_piece(q, choice):
            wanted = request_smem[q, 0, choice]
            top = jnp.logical_and(layer == LAYERS - 1, wanted < (LAYERS - 1) * SIDE)
            return stores[g][jnp.where(top, q + SIDE * (1 - choice), wanted)]

        for offset in range(1, SIDE):
            for choice in range(2):
                piece = wanted_piece((place + offset) % SIDE, choice)
                outgoing[g][offset - 1, :, choice] = piece
            deliver(g, offset).start()
        for choice in range(2):
            gathered[g][:, 1 + choice, pl.ds(place * quarter, quarter), :] = wanted_piece(
                place, choice
            )

    def compute(g):
        for offset in range(1, SIDE):
            deliver(g, offset).wait_recv()

        def head(index, carry):
            column = pl.multiple_of((g * GROUP_WIDTH + index) * HEAD_SIZE, HEAD_SIZE)
            out_ref[:, pl.ds(column, HEAD_SIZE)] = attend_head(
                query_ref[:, pl.ds(column, HEAD_SIZE)],
                gathered[g][0].reshape(3 * rows, HEAD_SIZE),
                gathered[g][1].reshape(3 * rows, HEAD_SIZE),
                causal,
                first_valid,
                second_valid,
                rows,
            )
            return carry

        lax.fori_loop(0, GROUP_WIDTH, head, 0)

    for g in range(heads):
        wait_spread(g)
        pass_on(g)
        hand_out(g)
        if g > 0:
            compute(g - 1)
    compute(heads - 1)

    for offset in range(1, SIDE):
        request(offset).wait_send()

    @pl.when(layer == LAYERS - 1)
    def _():
        for offset in range(SIDE):
            request_down(offset).wait_send()

    for g in range(heads):
        for offset in range(1, SIDE):
            spread(g, offset).wait_send()
            deliver(g, offset).wait_send()

        @pl.when(layer == 0)
        def _():
            chain(g, 0, 0).wait_send()

        @pl.when(layer == 1)
        def _():
            chain(g, 1, 0).wait_send()
            chain(g, 0, 1).wait_send()

        @pl.when(layer == 2)
        def _():
            chain_top(g).wait_send()


def relayed(queries, all_key_states, all_value_states, selected):
    rows = queries.shape[0]
    quarter = rows // SIDE
    heads = KEY_VALUE_HEADS
    blocks = LAYERS * SIDE
    kind = all_key_states.dtype
    vmem = pl.BlockSpec(memory_space=pltpu.VMEM)
    dma = pltpu.SemaphoreType.DMA
    return pl.pallas_call(
        functools.partial(relay_kernel, rows),
        out_shape=jax.ShapeDtypeStruct(queries.shape, queries.dtype),
        in_specs=[pl.BlockSpec(memory_space=pltpu.SMEM), vmem, vmem, vmem],
        out_specs=vmem,
        scratch_shapes=[pltpu.VMEM((blocks, 2, quarter, HEAD_SIZE), kind)] * heads
        + [pltpu.VMEM((2, 3, rows, HEAD_SIZE), kind)] * heads
        + [pltpu.VMEM((2 * SIDE, 2, quarter, HEAD_SIZE), kind)] * heads
        + [pltpu.VMEM((SIDE - 1, 2, 2, quarter, HEAD_SIZE), kind)] * heads
        + [
            pltpu.VMEM((2 * SIDE, 1, 128), jnp.int32),
            pltpu.SMEM((2 * SIDE, 1, 128), jnp.int32),
            dma((2 * SIDE - 1,)),
            dma((2 * SIDE - 1,)),
            dma((heads, SIDE - 1)),
            dma((heads, SIDE - 1)),
            dma((heads, 2)),
            dma((heads, 2)),
            dma((heads, SIDE - 1)),
            dma((heads, SIDE - 1)),
            dma,
        ],
        compiler_params=pltpu.CompilerParams(
            collective_id=0, has_side_effects=True, vmem_limit_bytes=40 * 2**20
        ),
    )(selected, queries, all_key_states, all_value_states)


def attend_kernel(valid_ref, query_ref, key_ref, value_ref, out_ref):
    rows = query_ref.shape[0]
    causal = lax.broadcasted_iota(jnp.int32, (rows, rows), 1) <= lax.broadcasted_iota(
        jnp.int32, (rows, rows), 0
    )
    out_ref[...] = attend_head(
        query_ref[...],
        key_ref[...],
        value_ref[...],
        causal,
        valid_ref[0] != 0,
        valid_ref[1] != 0,
        rows,
    )


def exchanged(queries, all_key_states, all_value_states, selected):
    devices = lax.axis_size("ctx")
    me = lax.axis_index("ctx")
    rows, width = all_key_states.shape
    exchange = functools.partial(
        lax.all_to_all, axis_name="ctx", split_axis=0, concat_axis=0, tiled=True
    )
    both = jnp.concatenate([all_key_states, all_value_states], axis=1)
    requests = lax.all_gather(selected, "ctx", axis=0, tiled=True)
    held = exchange(both.reshape(devices, rows // devices, 2 * width))
    chosen = [
        exchange(jnp.take(held, requests[:, choice], axis=0)).reshape(rows, 2 * width)
        for choice in range(2)
    ]
    everything = jnp.concatenate([both] + chosen, axis=0)
    first, second = selected[0, 0], selected[0, 1]
    valid = jnp.stack([first < me, jnp.logical_and(second < me, second != first)])
    return pl.pallas_call(
        attend_kernel,
        out_shape=jax.ShapeDtypeStruct(queries.shape, queries.dtype),
        grid=(QUERY_HEADS,),
        in_specs=[
            pl.BlockSpec(memory_space=pltpu.SMEM),
            pl.BlockSpec((rows, HEAD_SIZE), lambda h: (0, h)),
            pl.BlockSpec((3 * rows, HEAD_SIZE), lambda h: (0, h // GROUP_WIDTH)),
            pl.BlockSpec((3 * rows, HEAD_SIZE), lambda h: (0, KEY_VALUE_HEADS + h // GROUP_WIDTH)),
        ],
        out_specs=pl.BlockSpec((rows, HEAD_SIZE), lambda h: (0, h)),
    )(valid.astype(jnp.int32), queries, everything, everything)


def solution(mesh):
    placed = P(("groups", "ctx"), None)
    local = relayed if mesh.shape["ctx"] == LAYERS * SIDE else exchanged
    return jax.shard_map(
        local, mesh=mesh, in_specs=(placed,) * 4, out_specs=placed, check_vma=False
    )
```

time: 137 us -> 57.1 us (0.42)
  blocking collectives: 57.3 us -> 0 us
  Pallas kernels: 0 us -> 51.1 us
  starting transfers between devices: 20.2 us -> 0 us
  matrix products: 20.1 us -> 0 us
  local copies, waits for them, and re-layouts: 18.8 us -> 5.47 us
  other arithmetic: 10.7 us -> 0 us
  waiting for transfers between devices: 5.45 us -> 0 us
  between operations: 2.63 us -> 0.01 us
    pallas_call x0 -> x1, Pallas kernels: none -> 51.1 us  [relayed(): pl.pallas_call(functools.partial(relay_kernel, rows), out_shape=jax.Shape...]
    all_to_all x3 -> x0, blocking collectives: 40 us -> none  [the longest x1 13.9 us: local(): lax.all_to_all(key_split, 'ctx', split_axis=0, concat_axis=0, tiled=True)]
    all_to_all x3 -> x0, starting transfers between devices: 20.2 us -> none  [the longest x1 8.15 us: local(): lax.all_to_all(jnp.take(held_keys, wanted[0], axis=0), 'ctx', split_axis=...]
    dot_general x8 -> x0, matrix products: 20.1 us -> none  [the longest x4 14.8 us: one_head(): jnp.einsum('tru,ud->trd', weights.astype(jnp.bfloat16), value_part, prefe...]
    all_gather x1 -> x0, blocking collectives: 17.3 us -> none  [local(): requests = lax.all_gather(selected, 'ctx', axis=0, tiled=True)]
    reduce_sum x4 -> x0, other arithmetic: 6.7 us -> none  [one_head(): row_sum = jnp.sum(weights, axis=2, keepdims=True)]
    concatenate x10 -> x0, local copies, waits for them, and re-layouts: 6.41 us -> none  [the longest x4 4.47 us: local(): jnp.concatenate([all_key_states, distant_keys], axis=0)]
    all_to_all x3 -> x0, waiting for transfers between devices: 5.45 us -> none  [the longest x1 5.45 us: local(): lax.all_to_all(jnp.take(held_keys, wanted[0], axis=0), 'ctx', split_axis=...]
  transfers between devices with their start and end apart: 3 -> 0, of which waited for: 1 -> 0; matrix products, arithmetic and copies ran while one was open for 10% -> 0% of each run, Pallas kernels for 0% -> 0%
where the time goes in v1:
time: 57.1 us; the launch traced here: 56.6 us
  Pallas kernels  51.1 us (89%)
  local copies, waits for them, and re-layouts  5.47 us (10%)
    pallas_call x1, Pallas kernels, relayed(): pl.pallas_call(functools.partial(relay_kernel, rows), out_shape=jax.Shape...  51.1 us
    unnamed x9, local copies, waits for them, and re-layouts  5.47 us

profile of v1, /device:TPU:25, one launch (start us, length us, event | category | flops | bytes accessed | tf_op | source)
XLA Modules:
  0.0 56.6 jit_solution(5551458323856406416)
XLA Ops:
  0.0 0.0 copy-start
  0.0 1.6 %copy-done = bf16[256,4096]{1,0:T(8,128)(2,1)S(1)} copy-done((bf16[256,4096]{1,0:T(8,128)(2,1)S(1)}, bf16[256,4096]{1,0:T(8,128)(2,1)}, u32[]{:S(2)}) %copy-start) | copy-done | bytes 2097176
  1.6 0.0 copy-start.1
  1.6 0.9 %copy-done.1 = bf16[256,512]{1,0:T(8,128)(2,1)S(1)} copy-done((bf16[256,512]{1,0:T(8,128)(2,1)S(1)}, bf16[256,512]{1,0:T(8,128)(2,1)}, u32[]{:S(2)}) %copy-start.1) | copy-done | bytes 262168
  2.5 0.0 copy-start.2
  2.5 0.9 %copy-done.2 = bf16[256,512]{1,0:T(8,128)(2,1)S(1)} copy-done((bf16[256,512]{1,0:T(8,128)(2,1)S(1)}, bf16[256,512]{1,0:T(8,128)(2,1)}, u32[]{:S(2)}) %copy-start.2) | copy-done | bytes 262168
  3.5 0.0 copy-start.3
  3.5 0.7 %copy-done.3 = s32[1,2]{1,0:T(1,128)S(1)} copy-done((s32[1,2]{1,0:T(1,128)S(1)}, s32[1,2]{1,0:T(1,128)}, u32[]{:S(2)}) %copy-start.3) | copy-done | bytes 32
  4.1 51.1 %shard_map.46 = bf16[256,4096]{1,0:T(8,128)(2,1)S(1)} custom-call(s32[1,2]{1,0:T(1,128)S(1)} %copy-done.3, bf16[256,4096]{1,0:T(8,128)(2,1)S(1)} %copy-done, bf16[256,512]{1,0:T(8,128)(2,1)S(1)} %copy-done.1, bf16[256,512]{1,0:T(8,128)(2,1)S(1)} %copy-done.2), custom_call_target="tpu_custom_call" | custom-call | tf_op jit(solution)/shard_map/pallas_call | solution.py:313
  55.3 1.3 %copy.6 = bf16[256,4096]{1,0:T(8,128)(2,1)} copy(bf16[256,4096]{1,0:T(8,128)(2,1)S(1)} %shard_map.46) | data formatting | bytes 4194304
Async XLA Ops:
  0.0 1.6 %copy-start = (bf16[256,4096]{1,0:T(8,128)(2,1)S(1)}, bf16[256,4096]{1,0:T(8,128)(2,1)}, u32[]{:S(2)}) copy-start(bf16[256,4096]{1,0:T(8,128)(2,1)} %query_ref.1) | copy-start | bytes 6291460
  1.6 0.9 %copy-start.1 = (bf16[256,512]{1,0:T(8,128)(2,1)S(1)}, bf16[256,512]{1,0:T(8,128)(2,1)}, u32[]{:S(2)}) copy-start(bf16[256,512]{1,0:T(8,128)(2,1)} %key_ref.1) | copy-start | bytes 786436
  2.5 0.9 %copy-start.2 = (bf16[256,512]{1,0:T(8,128)(2,1)S(1)}, bf16[256,512]{1,0:T(8,128)(2,1)}, u32[]{:S(2)}) copy-start(bf16[256,512]{1,0:T(8,128)(2,1)} %value_ref.1) | copy-start | bytes 786436
  3.5 0.7 %copy-start.3 = (s32[1,2]{1,0:T(1,128)S(1)}, s32[1,2]{1,0:T(1,128)}, u32[]{:S(2)}) copy-start(s32[1,2]{1,0:T(1,128)} %selected_ref.1) | copy-start | bytes 28

commit v2 on v1

--- a/solution.py
+++ b/solution.py
@@ -19,34 +19,52 @@
 MESH = pl.DeviceIdType.MESH
 
 
-def attend_head(queries, keys, values, causal, first_valid, second_valid, rows):
+def half_max(scores):
+    return jnp.maximum(scores[:, :HEAD_SIZE], scores[:, HEAD_SIZE:])
+
+
+def attend_head(queries, keys, values, causal, first_valid, second_valid):
+    rows = queries.shape[0]
     scores = lax.dot_general(
         queries, keys, (((1,), (1,)), ((), ())), preferred_element_type=jnp.float32
     )
     own = jnp.where(causal, scores[:, :rows], MASKED)
     first = scores[:, rows : 2 * rows]
     second = scores[:, 2 * rows :]
-    own_max = jnp.max(own, axis=1, keepdims=True)
-    first_max = jnp.where(first_valid, jnp.max(first, axis=1, keepdims=True), MASKED)
-    second_max = jnp.where(second_valid, jnp.max(second, axis=1, keepdims=True), MASKED)
-    row_max = jnp.maximum(own_max, jnp.maximum(first_max, second_max))
-    own = jnp.exp2((own - row_max) * EXPONENT_SCALE)
-    first = jnp.exp2((first - jnp.where(first_valid, row_max, -MASKED)) * EXPONENT_SCALE)
-    second = jnp.exp2((second - jnp.where(second_valid, row_max, -MASKED)) * EXPONENT_SCALE)
-    row_sum = jnp.sum(own + first + second, axis=1, keepdims=True)
+    row_max = jnp.max(
+        jnp.maximum(
+            half_max(own),
+            jnp.maximum(
+                jnp.where(first_valid, half_max(first), MASKED),
+                jnp.where(second_valid, half_max(second), MASKED),
+            ),
+        ),
+        axis=1,
+        keepdims=True,
+    )
+    first_max = jnp.where(first_valid, row_max, -MASKED)
+    second_max = jnp.where(second_valid, row_max, -MASKED)
     weights = jnp.concatenate(
-        [own.astype(jnp.bfloat16), first.astype(jnp.bfloat16), second.astype(jnp.bfloat16)], axis=1
+        [
+            jnp.exp2((part - top) * EXPONENT_SCALE).astype(jnp.bfloat16)
+            for part, top in ((own, row_max), (first, first_max), (second, second_max))
+        ],
+        axis=1,
     )
     mixture = jnp.dot(weights, values, preferred_element_type=jnp.float32)
-    return (mixture * (1.0 / row_sum)).astype(jnp.bfloat16)
+    return (mixture[:, :HEAD_SIZE] * (1.0 / mixture[:, HEAD_SIZE:])).astype(jnp.bfloat16)
+
+
+def with_ones(values):
+    return jnp.concatenate([values, jnp.ones_like(values)], axis=1)
 
 
 def relay_kernel(
     rows,
-    selected_ref,
-    query_ref,
-    key_ref,
-    value_ref,
+    selected_hbm,
+    query_hbm,
+    key_hbm,
+    value_hbm,
     out_ref,
     *scratch,
 ):
@@ -67,6 +85,11 @@
         deliver_send,
         deliver_recv,
         local_sem,
+        selected_ref,
+        query_ref,
+        selected_sem,
+        query_sem,
+        pack_sem,
     ) = scratch[4 * heads :]
     quarter = rows // SIDE
     me = lax.axis_index("ctx")
@@ -76,12 +99,27 @@
     def peer(offset):
         return layer * SIDE + (place + offset) % SIDE
 
+    def pack(g, which):
+        source = (key_hbm, value_hbm)[which]
+        return pltpu.make_async_copy(
+            source.at[:, pl.ds(g * HEAD_SIZE, HEAD_SIZE)],
+            gathered[g].at[which, 0],
+            pack_sem.at[g, which],
+        )
+
+    def fetch_queries(g):
+        columns = pl.ds(g * GROUP_WIDTH * HEAD_SIZE, GROUP_WIDTH * HEAD_SIZE)
+        return pltpu.make_async_copy(
+            query_hbm.at[:, columns], query_ref.at[:, columns], query_sem.at[g]
+        )
+
+    fetch_selected = pltpu.make_async_copy(selected_hbm, selected_ref, selected_sem)
+    fetch_selected.start()
     for g in range(heads):
-        columns = slice(g * HEAD_SIZE, (g + 1) * HEAD_SIZE)
-        gathered[g][0, 0] = key_ref[:, columns]
-        gathered[g][1, 0] = value_ref[:, columns]
-    lane = lax.broadcasted_iota(jnp.int32, (1, 128), 1)
-    request_vmem[place] = jnp.where(lane == 0, selected_ref[0, 0], selected_ref[0, 1])
+        for which in range(2):
+            pack(g, which).start()
+    for g in range(heads):
+        fetch_queries(g).start()
 
     barrier = pltpu.get_barrier_semaphore()
     for offset in range(1, SIDE):
@@ -103,6 +141,10 @@
 
     neighbour_layers = jnp.minimum(layer, 1) + jnp.minimum(LAYERS - 1 - layer, 1)
     pl.semaphore_wait(barrier, SIDE - 1 + SIDE * neighbour_layers)
+
+    fetch_selected.wait()
+    lane = lax.broadcasted_iota(jnp.int32, (1, 128), 1)
+    request_vmem[place] = jnp.where(lane == 0, selected_ref[0, 0], selected_ref[0, 1])
 
     def spread(g, offset):
         target = (place + offset) % SIDE
@@ -175,6 +217,8 @@
             request_down(offset).start()
 
     for g in range(heads):
+        for which in range(2):
+            pack(g, which).wait()
         for offset in range(1, SIDE):
             spread(g, offset).start()
         stores[g][me] = gathered[g][:, 0, pl.ds(place * quarter, quarter), :]
@@ -208,7 +252,7 @@
         for offset in range(1, SIDE):
             spread(g, offset).wait_recv()
 
-    def pass_on(g):
+    def pass_on_low(g):
         @pl.when(layer == 0)
         def _():
             chain(g, 0, 0).start()
@@ -219,6 +263,7 @@
             chain(g, 0, 0).wait_recv()
             chain(g, 0, 1).start()
 
+    def pass_on_high(g):
         @pl.when(layer == 2)
         def _():
             chain(g, 1, 0).wait_recv()
@@ -252,24 +297,28 @@
         for offset in range(1, SIDE):
             deliver(g, offset).wait_recv()
 
-        def head(index, carry):
-            column = pl.multiple_of((g * GROUP_WIDTH + index) * HEAD_SIZE, HEAD_SIZE)
-            out_ref[:, pl.ds(column, HEAD_SIZE)] = attend_head(
-                query_ref[:, pl.ds(column, HEAD_SIZE)],
-                gathered[g][0].reshape(3 * rows, HEAD_SIZE),
-                gathered[g][1].reshape(3 * rows, HEAD_SIZE),
-                causal,
-                first_valid,
-                second_valid,
-                rows,
+        fetch_queries(g).wait()
+        keys = gathered[g][0].reshape(3 * rows, HEAD_SIZE)
+        values = with_ones(gathered[g][1].reshape(3 * rows, HEAD_SIZE))
+        for index in range(GROUP_WIDTH):
+            columns = pl.ds((g * GROUP_WIDTH + index) * HEAD_SIZE, HEAD_SIZE)
+            out_ref[:, columns] = attend_head(
+                query_ref[:, columns], keys, values, causal, first_valid, second_valid
             )
-            return carry
-
-        lax.fori_loop(0, GROUP_WIDTH, head, 0)
+
+    @pl.when(layer < LAYERS - 2)
+    def _():
+        for g in range(heads):
+            wait_spread(g)
+            pass_on_low(g)
 
     for g in range(heads):
-        wait_spread(g)
-        pass_on(g)
+
+        @pl.when(layer >= LAYERS - 2)
+        def _():
+            wait_spread(g)
+            pass_on_high(g)
+
         hand_out(g)
         if g > 0:
             compute(g - 1)
@@ -313,7 +362,7 @@
     return pl.pallas_call(
         functools.partial(relay_kernel, rows),
         out_shape=jax.ShapeDtypeStruct(queries.shape, queries.dtype),
-        in_specs=[pl.BlockSpec(memory_space=pltpu.SMEM), vmem, vmem, vmem],
+        in_specs=[pl.BlockSpec(memory_space=pl.ANY)] * 4,
         out_specs=vmem,
         scratch_shapes=[pltpu.VMEM((blocks, 2, quarter, HEAD_SIZE), kind)] * heads
         + [pltpu.VMEM((2, 3, rows, HEAD_SIZE), kind)] * heads
@@ -331,9 +380,14 @@
             dma((heads, SIDE - 1)),
             dma((heads, SIDE - 1)),
             dma,
+            pltpu.SMEM((1, 2), jnp.int32),
+            pltpu.VMEM(queries.shape, queries.dtype),
+            dma,
+            dma((heads,)),
+            dma((heads, 2)),
         ],
         compiler_params=pltpu.CompilerParams(
-            collective_id=0, has_side_effects=True, vmem_limit_bytes=40 * 2**20
+            collective_id=0, has_side_effects=True, vmem_limit_bytes=60 * 2**20
         ),
     )(selected, queries, all_key_states, all_value_states)
 
@@ -346,11 +400,10 @@
     out_ref[...] = attend_head(
         query_ref[...],
         key_ref[...],
-        value_ref[...],
+        with_ones(value_ref[...]),
         causal,
         valid_ref[0] != 0,
         valid_ref[1] != 0,
-        rows,
     )
 
 

time: 57.1 us -> 48.8 us (0.85)
  Pallas kernels: 51.1 us -> 45.5 us
  local copies, waits for them, and re-layouts: 5.47 us -> 3.13 us
    pallas_call x1, Pallas kernels: 51.1 us -> 45.5 us  [relayed(): pl.pallas_call(functools.partial(relay_kernel, rows), out_shape=jax.Shape...]
    unnamed x9 -> x1, local copies, waits for them, and re-layouts: 5.47 us -> 3.13 us
where the time goes in v2:
time: 48.8 us; the launch traced here: 48.7 us
  Pallas kernels  45.5 us (93%)
  local copies, waits for them, and re-layouts  3.13 us (6%)
    pallas_call x1, Pallas kernels, relayed(): pl.pallas_call(functools.partial(relay_kernel, rows), out_shape=jax.Shape...  45.5 us
    unnamed x1, local copies, waits for them, and re-layouts  3.13 us

profile of v2, /device:TPU:25, one launch (start us, length us, event | category | flops | bytes accessed | tf_op | source)
XLA Modules:
  0.0 48.7 jit_solution(15666998562916853673)
XLA Ops:
  0.0 45.5 %shard_map.46 = bf16[256,4096]{1,0:T(8,128)(2,1)} custom-call(s32[1,2]{1,0:T(1,128)} %selected_hbm.1, bf16[256,4096]{1,0:T(8,128)(2,1)} %query_hbm.1, bf16[256,512]{1,0:T(8,128)(2,1)} %key_hbm.1, bf16[256,512]{1,0:T(8,128)(2,1)} %value_hbm.1), custom_call_target="tpu_custom_call" | custom-call | tf_op jit(solution)/shard_map/pallas_call | solution.py:362
  45.5 3.1 %copy.6 = bf16[256,4096]{1,0:T(8,128)(2,1)} copy(bf16[256,4096]{1,0:T(8,128)(2,1)} %shard_map.46) | data formatting | bytes 4194304

commit v3 on v2

--- a/solution.py
+++ b/solution.py
@@ -65,14 +65,17 @@
     query_hbm,
     key_hbm,
     value_hbm,
-    out_ref,
+    early_hbm,
+    last_keys,
+    last_values,
     *scratch,
 ):
     heads = KEY_VALUE_HEADS
-    stores = scratch[:heads]
-    gathered = scratch[heads : 2 * heads]
-    upward = scratch[2 * heads : 3 * heads]
-    outgoing = scratch[3 * heads : 4 * heads]
+    chunks = 2 * heads
+    stores = scratch[:chunks]
+    upward = scratch[chunks : 2 * chunks]
+    outgoing = scratch[2 * chunks : 3 * chunks]
+    gathered = scratch[3 * chunks : 4 * chunks - 2] + (last_keys, last_values)
     (
         request_vmem,
         request_smem,
@@ -90,7 +93,9 @@
         selected_sem,
         query_sem,
         pack_sem,
-    ) = scratch[4 * heads :]
+        early_ref,
+        early_sem,
+    ) = scratch[4 * chunks - 2 :]
     quarter = rows // SIDE
     me = lax.axis_index("ctx")
     layer = me // SIDE
@@ -99,12 +104,12 @@
     def peer(offset):
         return layer * SIDE + (place + offset) % SIDE
 
-    def pack(g, which):
-        source = (key_hbm, value_hbm)[which]
+    def pack(c):
+        source = (key_hbm, value_hbm)[c % 2]
         return pltpu.make_async_copy(
-            source.at[:, pl.ds(g * HEAD_SIZE, HEAD_SIZE)],
-            gathered[g].at[which, 0],
-            pack_sem.at[g, which],
+            source.at[:, pl.ds(c // 2 * HEAD_SIZE, HEAD_SIZE)],
+            gathered[c].at[0],
+            pack_sem.at[c],
         )
 
     def fetch_queries(g):
@@ -115,10 +120,9 @@
 
     fetch_selected = pltpu.make_async_copy(selected_hbm, selected_ref, selected_sem)
     fetch_selected.start()
-    for g in range(heads):
-        for which in range(2):
-            pack(g, which).start()
-    for g in range(heads):
+    for c in range(chunks):
+        pack(c).start()
+    for g in range(heads - 1):
         fetch_queries(g).start()
 
     barrier = pltpu.get_barrier_semaphore()
@@ -149,7 +153,7 @@
     def spread(g, offset):
         target = (place + offset) % SIDE
         return pltpu.make_async_remote_copy(
-            src_ref=gathered[g].at[:, 0, pl.ds(target * quarter, quarter), :],
+            src_ref=gathered[g].at[0, pl.ds(target * quarter, quarter), :],
             dst_ref=stores[g].at[me],
             send_sem=spread_send.at[g, offset - 1],
             recv_sem=spread_recv.at[g, offset - 1],
@@ -201,7 +205,7 @@
     def deliver(g, offset):
         return pltpu.make_async_remote_copy(
             src_ref=outgoing[g].at[offset - 1],
-            dst_ref=gathered[g].at[:, pl.ds(1, 2), pl.ds(place * quarter, quarter), :],
+            dst_ref=gathered[g].at[pl.ds(1, 2), pl.ds(place * quarter, quarter), :],
             send_sem=deliver_send.at[g, offset - 1],
             recv_sem=deliver_recv.at[g, offset - 1],
             device_id={"ctx": peer(offset)},
@@ -216,12 +220,11 @@
         for offset in range(SIDE):
             request_down(offset).start()
 
-    for g in range(heads):
-        for which in range(2):
-            pack(g, which).wait()
+    for c in range(chunks):
+        pack(c).wait()
         for offset in range(1, SIDE):
-            spread(g, offset).start()
-        stores[g][me] = gathered[g][:, 0, pl.ds(place * quarter, quarter), :]
+            spread(c, offset).start()
+        stores[c][me] = gathered[c][0, pl.ds(place * quarter, quarter), :]
 
     for offset in range(1, SIDE):
         request(offset).wait_recv()
@@ -259,7 +262,11 @@
 
         @pl.when(layer == 1)
         def _():
-            chain(g, 1, 0).start()
+            if g == 0:
+                chain(g, 1, 0).start()
+            if g + 1 < chunks:
+                wait_spread(g + 1)
+                chain(g + 1, 1, 0).start()
             chain(g, 0, 0).wait_recv()
             chain(g, 0, 1).start()
 
@@ -286,43 +293,61 @@
         for offset in range(1, SIDE):
             for choice in range(2):
                 piece = wanted_piece((place + offset) % SIDE, choice)
-                outgoing[g][offset - 1, :, choice] = piece
+                outgoing[g][offset - 1, choice] = piece
             deliver(g, offset).start()
         for choice in range(2):
-            gathered[g][:, 1 + choice, pl.ds(place * quarter, quarter), :] = wanted_piece(
+            gathered[g][1 + choice, pl.ds(place * quarter, quarter), :] = wanted_piece(
                 place, choice
             )
 
     def compute(g):
-        for offset in range(1, SIDE):
-            deliver(g, offset).wait_recv()
-
+        for c in (2 * g, 2 * g + 1):
+            for offset in range(1, SIDE):
+                deliver(c, offset).wait_recv()
         fetch_queries(g).wait()
-        keys = gathered[g][0].reshape(3 * rows, HEAD_SIZE)
-        values = with_ones(gathered[g][1].reshape(3 * rows, HEAD_SIZE))
+        keys = gathered[2 * g][...].reshape(3 * rows, HEAD_SIZE)
+        values = with_ones(gathered[2 * g + 1][...].reshape(3 * rows, HEAD_SIZE))
         for index in range(GROUP_WIDTH):
             columns = pl.ds((g * GROUP_WIDTH + index) * HEAD_SIZE, HEAD_SIZE)
-            out_ref[:, columns] = attend_head(
+            early_ref[:, columns] = attend_head(
                 query_ref[:, columns], keys, values, causal, first_valid, second_valid
             )
 
-    @pl.when(layer < LAYERS - 2)
-    def _():
-        for g in range(heads):
-            wait_spread(g)
-            pass_on_low(g)
-
-    for g in range(heads):
+        write_early(g).start()
+
+    def write_early(g):
+        columns = pl.ds(g * GROUP_WIDTH * HEAD_SIZE, GROUP_WIDTH * HEAD_SIZE)
+        return pltpu.make_async_copy(
+            early_ref.at[:, columns], early_hbm.at[:, columns], early_sem.at[g]
+        )
+
+    @pl.when(layer == 0)
+    def _():
+        for c in range(chunks):
+            wait_spread(c)
+            pass_on_low(c)
+
+    @pl.when(layer == 1)
+    def _():
+        wait_spread(0)
+        for c in range(chunks):
+            pass_on_low(c)
+
+    for c in range(chunks):
 
         @pl.when(layer >= LAYERS - 2)
         def _():
-            wait_spread(g)
-            pass_on_high(g)
-
-        hand_out(g)
-        if g > 0:
-            compute(g - 1)
-    compute(heads - 1)
+            wait_spread(c)
+            pass_on_high(c)
+
+        hand_out(c)
+        if c % 2 == 1 and c > 1:
+            compute(c // 2 - 1)
+    for c in (chunks - 2, chunks - 1):
+        for offset in range(1, SIDE):
+            deliver(c, offset).wait_recv()
+    for g in range(heads - 1):
+        write_early(g).wait()
 
     for offset in range(1, SIDE):
         request(offset).wait_send()
@@ -332,7 +357,7 @@
         for offset in range(SIDE):
             request_down(offset).wait_send()
 
-    for g in range(heads):
+    for g in range(chunks):
         for offset in range(1, SIDE):
             spread(g, offset).wait_send()
             deliver(g, offset).wait_send()
@@ -349,47 +374,113 @@
         @pl.when(layer == 2)
         def _():
             chain_top(g).wait_send()
+
+
+def finish_kernel(
+    selected_ref, query_ref, key_ref, value_ref, early_hbm, out_hbm, last_ref, early_sem, last_sem
+):
+    rows = query_ref.shape[0]
+    early = early_hbm.shape[1]
+    me = lax.axis_index("ctx")
+    early_copy = pltpu.make_async_copy(early_hbm, out_hbm.at[:, pl.ds(0, early)], early_sem)
+    early_copy.start()
+    first_valid = selected_ref[0, 0] < me
+    second_valid = jnp.logical_and(
+        selected_ref[0, 1] < me, selected_ref[0, 1] != selected_ref[0, 0]
+    )
+    causal = lax.broadcasted_iota(jnp.int32, (rows, rows), 1) <= lax.broadcasted_iota(
+        jnp.int32, (rows, rows), 0
+    )
+    keys = key_ref[...].reshape(3 * rows, HEAD_SIZE)
+    values = with_ones(value_ref[...].reshape(3 * rows, HEAD_SIZE))
+    writes = []
+    for pair in range(GROUP_WIDTH // 2):
+        for index in (2 * pair, 2 * pair + 1):
+            columns = pl.ds(index * HEAD_SIZE, HEAD_SIZE)
+            last_ref[:, columns] = attend_head(
+                query_ref[:, columns], keys, values, causal, first_valid, second_valid
+            )
+        writes.append(
+            pltpu.make_async_copy(
+                last_ref.at[:, pl.ds(2 * pair * HEAD_SIZE, 2 * HEAD_SIZE)],
+                out_hbm.at[:, pl.ds(early + 2 * pair * HEAD_SIZE, 2 * HEAD_SIZE)],
+                last_sem.at[pair],
+            )
+        )
+        writes[-1].start()
+    for write in writes:
+        write.wait()
+    early_copy.wait()
 
 
 def relayed(queries, all_key_states, all_value_states, selected):
     rows = queries.shape[0]
     quarter = rows // SIDE
     heads = KEY_VALUE_HEADS
+    chunks = 2 * heads
     blocks = LAYERS * SIDE
     kind = all_key_states.dtype
+    early = queries.shape[1] - GROUP_WIDTH * HEAD_SIZE
     vmem = pl.BlockSpec(memory_space=pltpu.VMEM)
+    anywhere = pl.BlockSpec(memory_space=pl.ANY)
     dma = pltpu.SemaphoreType.DMA
-    return pl.pallas_call(
+    attended_early, last_keys, last_values = pl.pallas_call(
         functools.partial(relay_kernel, rows),
-        out_shape=jax.ShapeDtypeStruct(queries.shape, queries.dtype),
-        in_specs=[pl.BlockSpec(memory_space=pl.ANY)] * 4,
-        out_specs=vmem,
-        scratch_shapes=[pltpu.VMEM((blocks, 2, quarter, HEAD_SIZE), kind)] * heads
-        + [pltpu.VMEM((2, 3, rows, HEAD_SIZE), kind)] * heads
-        + [pltpu.VMEM((2 * SIDE, 2, quarter, HEAD_SIZE), kind)] * heads
-        + [pltpu.VMEM((SIDE - 1, 2, 2, quarter, HEAD_SIZE), kind)] * heads
+        out_shape=(
+            jax.ShapeDtypeStruct((rows, early), queries.dtype),
+            jax.ShapeDtypeStruct((3, rows, HEAD_SIZE), kind),
+            jax.ShapeDtypeStruct((3, rows, HEAD_SIZE), kind),
+        ),
+        in_specs=[anywhere] * 4,
+        out_specs=(anywhere, vmem, vmem),
+        scratch_shapes=[pltpu.VMEM((blocks, quarter, HEAD_SIZE), kind)] * chunks
+        + [pltpu.VMEM((2 * SIDE, quarter, HEAD_SIZE), kind)] * chunks
+        + [pltpu.VMEM((SIDE - 1, 2, quarter, HEAD_SIZE), kind)] * chunks
+        + [pltpu.VMEM((3, rows, HEAD_SIZE), kind)] * (chunks - 2)
         + [
             pltpu.VMEM((2 * SIDE, 1, 128), jnp.int32),
             pltpu.SMEM((2 * SIDE, 1, 128), jnp.int32),
             dma((2 * SIDE - 1,)),
             dma((2 * SIDE - 1,)),
-            dma((heads, SIDE - 1)),
-            dma((heads, SIDE - 1)),
-            dma((heads, 2)),
-            dma((heads, 2)),
-            dma((heads, SIDE - 1)),
-            dma((heads, SIDE - 1)),
+            dma((chunks, SIDE - 1)),
+            dma((chunks, SIDE - 1)),
+            dma((chunks, 2)),
+            dma((chunks, 2)),
+            dma((chunks, SIDE - 1)),
+            dma((chunks, SIDE - 1)),
             dma,
             pltpu.SMEM((1, 2), jnp.int32),
-            pltpu.VMEM(queries.shape, queries.dtype),
+            pltpu.VMEM((rows, early), queries.dtype),
             dma,
-            dma((heads,)),
-            dma((heads, 2)),
+            dma((heads - 1,)),
+            dma((chunks,)),
+            pltpu.VMEM((rows, early), queries.dtype),
+            dma((heads - 1,)),
         ],
         compiler_params=pltpu.CompilerParams(
             collective_id=0, has_side_effects=True, vmem_limit_bytes=60 * 2**20
         ),
     )(selected, queries, all_key_states, all_value_states)
+    width = GROUP_WIDTH * HEAD_SIZE
+    return pl.pallas_call(
+        finish_kernel,
+        out_shape=jax.ShapeDtypeStruct(queries.shape, queries.dtype),
+        grid=(1,),
+        in_specs=[
+            pl.BlockSpec(memory_space=pltpu.SMEM),
+            pl.BlockSpec((rows, width), lambda i: (0, early // width)),
+            pl.BlockSpec((3, rows, HEAD_SIZE), lambda i: (0, 0, 0)),
+            pl.BlockSpec((3, rows, HEAD_SIZE), lambda i: (0, 0, 0)),
+            anywhere,
+        ],
+        out_specs=anywhere,
+        scratch_shapes=[
+            pltpu.VMEM((rows, width), queries.dtype),
+            dma,
+            dma((GROUP_WIDTH // 2,)),
+        ],
+        compiler_params=pltpu.CompilerParams(vmem_limit_bytes=60 * 2**20),
+    )(selected, queries, last_keys, last_values, attended_early)
 
 
 def attend_kernel(valid_ref, query_ref, key_ref, value_ref, out_ref):

time: 48.8 us -> 90.4 us (1.85)
  Pallas kernels: 45.5 us -> 90.2 us
  local copies, waits for them, and re-layouts: 3.13 us -> 0 us
    pallas_call x1 -> x2, Pallas kernels: 45.5 us -> 90.2 us  [the longest x1 50 us: relayed(): pl.pallas_call(finish_kernel, out_shape=jax.ShapeDtypeStruct(queries.shap...]
    unnamed x1 -> x0, local copies, waits for them, and re-layouts: 3.13 us -> none
where the time goes in v3:
time: 90.4 us; the launch traced here: 90.2 us
  Pallas kernels  90.2 us (100%)
    pallas_call x1, Pallas kernels, relayed(): pl.pallas_call(finish_kernel, out_shape=jax.ShapeDtypeStruct(queries.shap...  50 us
    pallas_call x1, Pallas kernels, relayed(): pl.pallas_call(functools.partial(relay_kernel, rows), out_shape=(jax.Shap...  40.2 us

profile of v3, /device:TPU:25, one launch (start us, length us, event | category | flops | bytes accessed | tf_op | source)
XLA Modules:
  0.0 90.2 jit_solution(1956449245530795470)
XLA Ops:
  0.0 40.2 %shard_map.46 = (bf16[256,3072]{1,0:T(8,128)(2,1)}, bf16[3,256,128]{2,1,0:T(8,128)(2,1)}, bf16[3,256,128]{2,1,0:T(8,128)(2,1)}) custom-call(s32[1,2]{1,0:T(1,128)} %selected_ref.1, bf16[256,4096]{1,0:T(8,128)(2,1)} %query_ref.1, bf16[256,512]{1,0:T(8,128)(2,1)} %key_hbm.1, bf16[256,512]{1,0:T(8,128)(2,1)} %value_hbm.1), custom_call_target="tpu_custom_call" | custom-call | tf_op jit(solution)/shard_map/pallas_call | solution.py:427
  40.2 50.0 %shard_map.47 = bf16[256,4096]{1,0:T(8,128)(2,1)} custom-call(s32[1,2]{1,0:T(1,128)} %selected_ref.1, bf16[256,4096]{1,0:T(8,128)(2,1)} %query_ref.1, bf16[3,256,128]{2,1,0:T(8,128)(2,1)} %get-tuple-element.8.key_ref, bf16[3,256,128]{2,1,0:T(8,128)(2,1)} %get-tuple-element.9.value_ref, bf16[256,3072]{1,0:T(8,128)(2,1)} %get-tuple-element.10.early_hbm), custom_call_target="tpu_custom_call" | custom-call | tf_op jit(solution)/shard_map/pallas_call | solution.py:465

commit v4 on v3

--- a/solution.py
+++ b/solution.py
@@ -333,16 +333,28 @@
         for c in range(chunks):
             pass_on_low(c)
 
+    @pl.when(layer < LAYERS - 1)
+    def _():
+        for c in range(chunks):
+
+            @pl.when(layer == LAYERS - 2)
+            def _():
+                wait_spread(c)
+                pass_on_high(c)
+
+            hand_out(c)
+
     for c in range(chunks):
 
-        @pl.when(layer >= LAYERS - 2)
+        @pl.when(layer == LAYERS - 1)
         def _():
             wait_spread(c)
             pass_on_high(c)
-
-        hand_out(c)
+            hand_out(c)
+
         if c % 2 == 1 and c > 1:
             compute(c // 2 - 1)
+
     for c in (chunks - 2, chunks - 1):
         for offset in range(1, SIDE):
             deliver(c, offset).wait_recv()
@@ -377,13 +389,25 @@
 
 
 def finish_kernel(
-    selected_ref, query_ref, key_ref, value_ref, early_hbm, out_hbm, last_ref, early_sem, last_sem
+    selected_ref,
+    query_ref,
+    key_ref,
+    value_ref,
+    early_hbm,
+    out_hbm,
+    last_ref,
+    early_ref,
+    early_sem,
+    last_sem,
 ):
     rows = query_ref.shape[0]
     early = early_hbm.shape[1]
     me = lax.axis_index("ctx")
-    early_copy = pltpu.make_async_copy(early_hbm, out_hbm.at[:, pl.ds(0, early)], early_sem)
-    early_copy.start()
+    early_in = pltpu.make_async_copy(early_hbm, early_ref, early_sem.at[0])
+    early_in.start()
+    early_out = pltpu.make_async_copy(
+        early_ref, out_hbm.at[:, pl.ds(0, early)], early_sem.at[1]
+    )
     first_valid = selected_ref[0, 0] < me
     second_valid = jnp.logical_and(
         selected_ref[0, 1] < me, selected_ref[0, 1] != selected_ref[0, 0]
@@ -408,9 +432,12 @@
             )
         )
         writes[-1].start()
+        if pair == 0:
+            early_in.wait()
+            early_out.start()
     for write in writes:
         write.wait()
-    early_copy.wait()
+    early_out.wait()
 
 
 def relayed(queries, all_key_states, all_value_states, selected):
@@ -476,7 +503,8 @@
         out_specs=anywhere,
         scratch_shapes=[
             pltpu.VMEM((rows, width), queries.dtype),
-            dma,
+            pltpu.VMEM((rows, early), queries.dtype),
+            dma((2,)),
             dma((GROUP_WIDTH // 2,)),
         ],
         compiler_params=pltpu.CompilerParams(vmem_limit_bytes=60 * 2**20),

time: 90.4 us -> 45.5 us (0.50)
  Pallas kernels: 90.2 us -> 45.3 us
    pallas_call x1, Pallas kernels: 50 us -> 5.13 us  [relayed(): pl.pallas_call(finish_kernel, out_shape=jax.ShapeDtypeStruct(queries.shap...]
where the time goes in v4:
time: 45.5 us; the launch traced here: 45.3 us
  Pallas kernels  45.3 us (100%)
    pallas_call x1, Pallas kernels, relayed(): pl.pallas_call(functools.partial(relay_kernel, rows), out_shape=(jax.Shap...  40.2 us
    pallas_call x1, Pallas kernels, relayed(): pl.pallas_call(finish_kernel, out_shape=jax.ShapeDtypeStruct(queries.shap...  5.13 us

profile of v4, /device:TPU:25, one launch (start us, length us, event | category | flops | bytes accessed | tf_op | source)
XLA Modules:
  0.0 45.3 jit_solution(12483565793783391900)
XLA Ops:
  0.0 40.2 %shard_map.46 = (bf16[256,3072]{1,0:T(8,128)(2,1)}, bf16[3,256,128]{2,1,0:T(8,128)(2,1)}, bf16[3,256,128]{2,1,0:T(8,128)(2,1)}) custom-call(s32[1,2]{1,0:T(1,128)} %selected_ref.1, bf16[256,4096]{1,0:T(8,128)(2,1)} %query_ref.1, bf16[256,512]{1,0:T(8,128)(2,1)} %key_hbm.1, bf16[256,512]{1,0:T(8,128)(2,1)} %value_hbm.1), custom_call_target="tpu_custom_call" | custom-call | tf_op jit(solution)/shard_map/pallas_call | solution.py:454
  40.2 5.1 %shard_map.47 = bf16[256,4096]{1,0:T(8,128)(2,1)} custom-call(s32[1,2]{1,0:T(1,128)} %selected_ref.1, bf16[256,4096]{1,0:T(8,128)(2,1)} %query_ref.1, bf16[3,256,128]{2,1,0:T(8,128)(2,1)} %get-tuple-element.8.key_ref, bf16[3,256,128]{2,1,0:T(8,128)(2,1)} %get-tuple-element.9.value_ref, bf16[256,3072]{1,0:T(8,128)(2,1)} %get-tuple-element.10.early_hbm), custom_call_target="tpu_custom_call" | custom-call | tf_op jit(solution)/shard_map/pallas_call | solution.py:492

commit v5 on v4

--- a/solution.py
+++ b/solution.py
@@ -16,6 +16,7 @@
 MASKED = -1e30
 LAYERS = 4
 SIDE = 4
+AHEAD = 3
 MESH = pl.DeviceIdType.MESH
 
 
@@ -222,8 +223,9 @@
 
     for c in range(chunks):
         pack(c).wait()
-        for offset in range(1, SIDE):
-            spread(c, offset).start()
+        if c < AHEAD:
+            for offset in range(1, SIDE):
+                spread(c, offset).start()
         stores[c][me] = gathered[c][0, pl.ds(place * quarter, quarter), :]
 
     for offset in range(1, SIDE):
@@ -254,16 +256,25 @@
     def wait_spread(g):
         for offset in range(1, SIDE):
             spread(g, offset).wait_recv()
+        if g + AHEAD < chunks:
+            for offset in range(1, SIDE):
+                spread(g + AHEAD, offset).start()
 
     def pass_on_low(g):
         @pl.when(layer == 0)
         def _():
+            if g > 1:
+                chain(g - 2, 0, 0).wait_send()
             chain(g, 0, 0).start()
 
         @pl.when(layer == 1)
         def _():
             if g == 0:
                 chain(g, 1, 0).start()
+            else:
+                chain(g - 1, 1, 0).wait_send()
+            if g > 1:
+                chain(g - 2, 0, 1).wait_send()
             if g + 1 < chunks:
                 wait_spread(g + 1)
                 chain(g + 1, 1, 0).start()
@@ -376,12 +387,15 @@
 
         @pl.when(layer == 0)
         def _():
-            chain(g, 0, 0).wait_send()
+            if g >= chunks - 2:
+                chain(g, 0, 0).wait_send()
 
         @pl.when(layer == 1)
         def _():
-            chain(g, 1, 0).wait_send()
-            chain(g, 0, 1).wait_send()
+            if g == chunks - 1:
+                chain(g, 1, 0).wait_send()
+            if g >= chunks - 2:
+                chain(g, 0, 1).wait_send()
 
         @pl.when(layer == 2)
         def _():

time: 45.5 us -> 46.8 us (1.029)
  the two profiles are of different devices: /device:TPU:25 before, /device:TPU:9 now
where the time goes in v5:
time: 46.8 us; the launch traced here: 46.6 us
  Pallas kernels  46.6 us (100%)
    pallas_call x1, Pallas kernels, relayed(): pl.pallas_call(functools.partial(relay_kernel, rows), out_shape=(jax.Shap...  41.5 us
    pallas_call x1, Pallas kernels, relayed(): pl.pallas_call(finish_kernel, out_shape=jax.ShapeDtypeStruct(queries.shap...  5.13 us

profile of v5, /device:TPU:9, one launch (start us, length us, event | category | flops | bytes accessed | tf_op | source)
XLA Modules:
  0.0 46.6 jit_solution(12871127918351206730)
XLA Ops:
  0.0 41.5 %shard_map.46 = (bf16[256,3072]{1,0:T(8,128)(2,1)}, bf16[3,256,128]{2,1,0:T(8,128)(2,1)}, bf16[3,256,128]{2,1,0:T(8,128)(2,1)}) custom-call(s32[1,2]{1,0:T(1,128)} %selected_ref.1, bf16[256,4096]{1,0:T(8,128)(2,1)} %query_ref.1, bf16[256,512]{1,0:T(8,128)(2,1)} %key_hbm.1, bf16[256,512]{1,0:T(8,128)(2,1)} %value_hbm.1), custom_call_target="tpu_custom_call" | custom-call | tf_op jit(solution)/shard_map/pallas_call | solution.py:468
  41.5 5.1 %shard_map.47 = bf16[256,4096]{1,0:T(8,128)(2,1)} custom-call(s32[1,2]{1,0:T(1,128)} %selected_ref.1, bf16[256,4096]{1,0:T(8,128)(2,1)} %query_ref.1, bf16[3,256,128]{2,1,0:T(8,128)(2,1)} %get-tuple-element.8.key_ref, bf16[3,256,128]{2,1,0:T(8,128)(2,1)} %get-tuple-element.9.value_ref, bf16[256,3072]{1,0:T(8,128)(2,1)} %get-tuple-element.10.early_hbm), custom_call_target="tpu_custom_call" | custom-call | tf_op jit(solution)/shard_map/pallas_call | solution.py:506

commit v6 on v4

--- a/solution.py
+++ b/solution.py
@@ -226,23 +226,6 @@
             spread(c, offset).start()
         stores[c][me] = gathered[c][0, pl.ds(place * quarter, quarter), :]
 
-    for offset in range(1, SIDE):
-        request(offset).wait_recv()
-
-    @pl.when(layer == LAYERS - 2)
-    def _():
-        for offset in range(SIDE):
-            request_down(offset).wait_recv()
-
-    @pl.when(layer != LAYERS - 2)
-    def _():
-        for q in range(SIDE):
-            request_vmem[SIDE + q] = jnp.zeros((1, 128), jnp.int32)
-
-    to_smem = pltpu.make_async_copy(request_vmem, request_smem, local_sem)
-    to_smem.start()
-    to_smem.wait()
-
     first_valid = selected_ref[0, 0] < me
     second_valid = jnp.logical_and(
         selected_ref[0, 1] < me, selected_ref[0, 1] != selected_ref[0, 0]
@@ -332,6 +315,23 @@
         wait_spread(0)
         for c in range(chunks):
             pass_on_low(c)
+
+    for offset in range(1, SIDE):
+        request(offset).wait_recv()
+
+    @pl.when(layer == LAYERS - 2)
+    def _():
+        for offset in range(SIDE):
+            request_down(offset).wait_recv()
+
+    @pl.when(layer != LAYERS - 2)
+    def _():
+        for q in range(SIDE):
+            request_vmem[SIDE + q] = jnp.zeros((1, 128), jnp.int32)
+
+    to_smem = pltpu.make_async_copy(request_vmem, request_smem, local_sem)
+    to_smem.start()
+    to_smem.wait()
 
     @pl.when(layer < LAYERS - 1)
     def _():

time: 45.5 us -> 45.2 us (level)
  no operation moved by 1% of the time
where the time goes in v6:
time: 45.2 us; the launch traced here: 45.1 us
  Pallas kernels  45.1 us (100%)
    pallas_call x1, Pallas kernels, relayed(): pl.pallas_call(functools.partial(relay_kernel, rows), out_shape=(jax.Shap...  39.9 us
    pallas_call x1, Pallas kernels, relayed(): pl.pallas_call(finish_kernel, out_shape=jax.ShapeDtypeStruct(queries.shap...  5.13 us

profile of v6, /device:TPU:25, one launch (start us, length us, event | category | flops | bytes accessed | tf_op | source)
XLA Modules:
  0.0 45.1 jit_solution(4303386347850905625)
XLA Ops:
  0.0 39.9 %shard_map.46 = (bf16[256,3072]{1,0:T(8,128)(2,1)}, bf16[3,256,128]{2,1,0:T(8,128)(2,1)}, bf16[3,256,128]{2,1,0:T(8,128)(2,1)}) custom-call(s32[1,2]{1,0:T(1,128)} %selected_ref.1, bf16[256,4096]{1,0:T(8,128)(2,1)} %query_ref.1, bf16[256,512]{1,0:T(8,128)(2,1)} %key_hbm.1, bf16[256,512]{1,0:T(8,128)(2,1)} %value_hbm.1), custom_call_target="tpu_custom_call" | custom-call | tf_op jit(solution)/shard_map/pallas_call | solution.py:454
  39.9 5.1 %shard_map.47 = bf16[256,4096]{1,0:T(8,128)(2,1)} custom-call(s32[1,2]{1,0:T(1,128)} %selected_ref.1, bf16[256,4096]{1,0:T(8,128)(2,1)} %query_ref.1, bf16[3,256,128]{2,1,0:T(8,128)(2,1)} %get-tuple-element.8.key_ref, bf16[3,256,128]{2,1,0:T(8,128)(2,1)} %get-tuple-element.9.value_ref, bf16[256,3072]{1,0:T(8,128)(2,1)} %get-tuple-element.10.early_hbm), custom_call_target="tpu_custom_call" | custom-call | tf_op jit(solution)/shard_map/pallas_call | solution.py:492
